TPU v7x, 256 devices: a whole 4x4x8 slice. The times are simulated.
256 devices in a mesh: segment: 8 (over y, z_lo), frame: 32 (over x, z_hi, core).
Axes of the slice: x: 4, y: 4, z: 8 (z_hi: 4, z_lo: 2; z = z_hi * 2 + z_lo), core: 2. Of those that a mesh axis runs over, the one named last changes fastest.
Arguments:
- noisy_clips: bfloat16 [4, 32, 16, 16, 512], P(None, 'frame'), may hold values from -6 to 6
- conv_first: bfloat16 [8, 9, 512, 512], P('segment', None, 'frame'), may hold values from -0.09375 to 0.09375
- conv_second: bfloat16 [8, 9, 512, 512], P('segment', None, 'frame'), may hold values from -0.09375 to 0.09375
- temporal: bfloat16 [8, 3, 512, 512], P('segment', None, 'frame'), may hold values from -0.15625 to 0.15625
Outputs:
- denoised: bfloat16 [4, 32, 16, 16, 512], P(None, 'frame', 'segment')
All inputs are finite; a program needn't handle non-finite values.
Results may differ from a plain program's by a relative error of at most 0.013.
Values may be sent and summed in bfloat16 or wider, within the bound.
No kernel may reach another device: no remote copies, remote signals or barrier semaphores. Data moves between devices by JAX's collectives and lax.ppermute only.
A program may use at most 64 MiB of HBM per device.

v0:
```python
import jax
import jax.numpy as jnp
from jax import lax
from jax.sharding import PartitionSpec as P

skip_scale = 0.7071067811865476


def passed_along(shard, axis, by):
    length = lax.axis_size(axis)
    pairs = [(i, i + by) for i in range(length) if 0 <= i + by < length]
    return lax.ppermute(shard, axis, pairs)


def partner(shard, axis, bit):
    return lax.ppermute(shard, axis, [(i, i ^ 1 << bit) for i in range(lax.axis_size(axis))])


def extended_2(cells, sides, width):
    for axis, dim in sides:
        count = lax.axis_size(axis)
        ends = count - 1
        head = lax.slice_in_dim(cells, 0, width, axis=dim)
        tail = lax.slice_in_dim(cells, cells.shape[dim] - width, cells.shape[dim], axis=dim)
        cells = jnp.concatenate(
            [
                lax.ppermute(tail, axis, [(i, (i + 1) % count) for i in range(ends)]),
                cells,
                lax.ppermute(head, axis, [((i + 1) % count, i) for i in range(ends)]),
            ],
            axis=dim,
        )
    return cells


def broadcast(shard, axis, root):
    mine = lax.axis_index(axis) == root
    return lax.psum(jnp.where(mine, shard, jnp.zeros_like(shard)), axis)


def spatial(field_in, kernel):
    extent = field_in.shape[1]
    channels = field_in.shape[3]
    padded = jnp.pad(field_in, ((0, 0), (1, 1), (1, 1), (0, 0)))
    accumulated = jnp.zeros((field_in.shape[0] * extent * extent, channels), jnp.float32)
    for row_shift in range(3):
        for col_shift in range(3):
            window = padded[
                :, row_shift : row_shift + extent, col_shift : col_shift + extent, :
            ].reshape(-1, channels)
            accumulated = accumulated + jnp.dot(
                window, kernel[3 * row_shift + col_shift], preferred_element_type=jnp.float32
            )
    return accumulated.reshape(field_in.shape)


def temporal_mix(extended, kernel, frame_local):
    channels = extended.shape[3]
    out_shape = (frame_local,) + extended.shape[1:]
    accumulated = jnp.zeros(out_shape, jnp.float32)
    for offset in range(3):
        window = extended[offset : offset + frame_local].reshape(-1, channels)
        accumulated = accumulated + jnp.dot(
            window, kernel[offset], preferred_element_type=jnp.float32
        ).reshape(out_shape)
    return accumulated


def on_device(noisy_clips, conv_first, conv_second, temporal):
    sections = lax.axis_size("segment")
    segment_id = lax.axis_index("segment")
    first_full, second_full, time_full = (
        lax.all_gather(conv_first, "frame", axis=2, tiled=True),
        lax.all_gather(conv_second, "frame", axis=2, tiled=True),
        lax.all_gather(temporal, "frame", axis=2, tiled=True),
    )
    first_kernel = first_full[0]
    second_kernel = second_full[0]
    time_kernel = time_full[0]
    clip_count = noisy_clips.shape[0]
    frame_local = noisy_clips.shape[1]
    side_len = noisy_clips.shape[2]
    block_shape = noisy_clips.shape[1:]
    tick_count = clip_count + sections - 1
    half_sections = sections // 2
    is_up = segment_id >= half_sections
    side_store = jnp.zeros((clip_count,) + block_shape, jnp.bfloat16)
    out_store = jnp.zeros(noisy_clips.shape, jnp.bfloat16)
    prev_out = jnp.zeros(block_shape, jnp.bfloat16)

    def tick_step(carry, tick_index):
        prev_out, side_store, out_store = carry
        clip_now = tick_index - segment_id
        active = (clip_now >= 0) & (clip_now < clip_count)
        clip_slot = jnp.clip(clip_now, 0, clip_count - 1)
        own_input = lax.dynamic_index_in_dim(noisy_clips, clip_slot, 0, keepdims=False)
        received = passed_along(prev_out, "segment", 1)
        entering = jnp.where(segment_id == 0, own_input, received)
        mirrored = entering
        for bit_number in range(sections.bit_length() - 1):
            mirrored = partner(mirrored, "segment", bit_number)
        mirror_clip = tick_index - (sections - 1 - segment_id)
        written = (jnp.arange(clip_count) == mirror_clip) & is_up
        side_store = jnp.where(written[:, None, None, None, None], mirrored[None], side_store)
        skip_feature = lax.dynamic_index_in_dim(side_store, clip_slot, 0, keepdims=False)
        joined = (
            (entering.astype(jnp.float32) + skip_feature.astype(jnp.float32)) * skip_scale
        ).astype(jnp.bfloat16)
        section_in = jnp.where(is_up, joined, entering)
        activated = lax.cond(
            active,
            lambda: jax.nn.silu(spatial(section_in, first_kernel)).astype(jnp.bfloat16),
            lambda: jnp.zeros(block_shape, jnp.bfloat16),
        )
        extended = extended_2(activated, (("frame", 0),), 1)

        def second_pass():
            branch_sum = spatial(activated, second_kernel) + temporal_mix(
                extended, time_kernel, frame_local
            )
            return (section_in.astype(jnp.float32) + jax.nn.silu(branch_sum)).astype(jnp.bfloat16)

        section_out = lax.cond(active, second_pass, lambda: jnp.zeros(block_shape, jnp.bfloat16))
        finished = (jnp.arange(clip_count) == clip_slot) & active & (segment_id == sections - 1)
        out_store = jnp.where(finished[:, None, None, None, None], section_out[None], out_store)
        return ((section_out, side_store, out_store), None)

    final_carry, unused = lax.scan(
        tick_step, (prev_out, side_store, out_store), jnp.arange(tick_count, dtype=jnp.int32)
    )
    delivered = broadcast(final_carry[2], "segment", sections - 1)
    slab_rows = side_len // sections
    return lax.dynamic_slice_in_dim(delivered, segment_id * slab_rows, slab_rows, 2)


def solution(mesh):
    in_specs = (
        P(None, "frame", None, None, None),
        P("segment", None, "frame", None),
        P("segment", None, "frame", None),
        P("segment", None, "frame", None),
    )
    out_specs = P(None, "frame", "segment", None, None)
    return jax.shard_map(
        on_device, mesh=mesh, in_specs=in_specs, out_specs=out_specs, check_vma=False
    )
```

profile of v0, /device:TPU:2, one launch (start us, length us, event | category | flops | bytes accessed | tf_op | source)
XLA Modules:
  0.0 975.8 jit_solution(13421447813197799213)
XLA Ops:
  8.8 56.3 %all-gather.8.cloned.1.call-done = bf16[1,3,512,512]{3,2,1,0:T(8,128)(2,1)} async-done(((bf16[1,3,16,512]{3,2,1,0:T(8,128)(2,1)}), bf16[1,3,512,512]{3,2,1,0:T(8,128)(2,1)}) %all-gather.8.cloned.1.call-update) | async-done | bytes 1572880 | tf_op jit(solution)/shard_map/all_gather | solution.py:75
  65.1 63.4 %all-gather.4.cloned.1.call-done = bf16[1,9,512,512]{3,2,1,0:T(8,128)(2,1)} async-done(((bf16[1,9,16,512]{3,2,1,0:T(8,128)(2,1)}), bf16[1,9,512,512]{3,2,1,0:T(8,128)(2,1)}) %all-gather.4.cloned.1.call-update) | async-done | bytes 4718608 | tf_op jit(solution)/shard_map/all_gather | solution.py:73
  128.4 63.1 %all-gather.6.cloned.1.call-done = bf16[1,9,512,512]{3,2,1,0:T(8,128)(2,1)} async-done(((bf16[1,9,16,512]{3,2,1,0:T(8,128)(2,1)}), bf16[1,9,512,512]{3,2,1,0:T(8,128)(2,1)}) %all-gather.6.cloned.1.call-update) | async-done | bytes 4718608 | tf_op jit(solution)/shard_map/all_gather | solution.py:74
  192.3 682.3 %while.16 = (s32[]{:T(128)}, bf16[1,16,16,512]{3,2,1,0:T(8,128)(2,1)}, bf16[4,1,16,16,512]{4,3,2,1,0:T(8,128)(2,1)S(1)}, bf16[4,1,16,16,512]{4,3,2,1,0:T(8,128)(...) while((s32[]{:T(128)}, ...), condition=%wide.region_5.6_spmd.clone, body=%wide.region_0.5_spmd.clone.sunk | while | flops 2825650176 | bytes 99615424 | solution.py:128
  245.5 7.0 conditional.7
  270.5 7.6 collective-permute-done.2
  278.8 7.2 collective-permute-done.3
  307.3 7.0 conditional.7
  342.1 7.3 collective-permute-done.3
  370.6 7.0 conditional.7
  397.8 7.7 collective-permute-done.2
  406.1 7.2 collective-permute-done.3
  434.5 7.0 conditional.7
  468.4 7.5 collective-permute-done.3
  491.1 14.6 %collective-permute-start = (bf16[1,16,16,512]{3,2,1,0:T(8,128)(2,1)}, bf16[1,16,16,512]{3,2,1,0:T(8,128)(2,1)S(1)}, u32[]{:S(2)}, u32[]{:S(2)}) collective-permute-start(bf16[1,16,16,512]{3,2,1,0:T(8,128)(2,1)} %get-tuple-element.343), channel_id=1, source_target_pairs={{0,32},{32,64},{64,96},{96,128},{128,160},{160,192},{192,224},{1,3... | collective-permute-start | bytes 786440 | tf_op jit(solution)/shard_map/while/body/eval_jaxpr/ppermute | solution.py:12
  510.8 6.9 collective-permute-start.1
  531.0 7.2 collective-permute-done.3
  562.9 15.2 %collective-permute-start.1 = (bf16[1,16,16,512]{3,2,1,0:T(8,128)(2,1)S(1)}, bf16[1,16,16,512]{3,2,1,0:T(8,128)(2,1)S(1)}, u32[]{:S(2)}, u32[]{:S(2)}) collective-permute-start(bf16[1,16,16,512]{3,2,1,0:T(8,128)(2,1)S(1)} %bitcast_select_fusion.2), channel_id=1, source_target_pairs={{0,32},{32,0},{64,96},{96,64},{128,160},{160,128},{192,224},{224,1... | collective-permute-start | bytes 786440 | tf_op jit(solution)/shard_map/while/body/eval_jaxpr/ppermute | solution.py:16
  594.0 7.3 collective-permute-done.3
  637.9 11.0 %collective-permute-start.2 = (bf16[1,16,16,512]{3,2,1,0:T(8,128)(2,1)S(1)}, bf16[1,16,16,512]{3,2,1,0:T(8,128)(2,1)S(1)}, u32[]{:S(2)}, u32[]{:S(2)}) collective-permute-start(bf16[1,16,16,512]{3,2,1,0:T(8,128)(2,1)S(1)} %collective-permute-done.1), channel_id=1, source_target_pairs={{0,64},{32,96},{64,0},{96,32},{128,192},{160,224},{192,128},{224,1... | collective-permute-start | bytes 786440 | tf_op jit(solution)/shard_map/while/body/eval_jaxpr/ppermute | solution.py:16
  699.2 13.0 %collective-permute-start.2 = (bf16[1,16,16,512]{3,2,1,0:T(8,128)(2,1)S(1)}, bf16[1,16,16,512]{3,2,1,0:T(8,128)(2,1)S(1)}, u32[]{:S(2)}, u32[]{:S(2)}) collective-permute-start(bf16[1,16,16,512]{3,2,1,0:T(8,128)(2,1)S(1)} %collective-permute-done.1), channel_id=1, source_target_pairs={{0,64},{32,96},{64,0},{96,32},{128,192},{160,224},{192,128},{224,1... | collective-permute-start | bytes 786440 | tf_op jit(solution)/shard_map/while/body/eval_jaxpr/ppermute | solution.py:16
  767.6 19.2 %collective-permute-start.3 = (bf16[1,16,16,512]{3,2,1,0:T(8,128)(2,1)S(1)}, bf16[1,16,16,512]{3,2,1,0:T(8,128)(2,1)S(1)}, u32[]{:S(2)}, u32[]{:S(2)}) collective-permute-start(bf16[1,16,16,512]{3,2,1,0:T(8,128)(2,1)S(1)} %collective-permute-done.2), channel_id=1, source_target_pairs={{0,128},{32,160},{64,192},{96,224},{128,0},{160,32},{192,64},{224,... | collective-permute-start | bytes 786440 | tf_op jit(solution)/shard_map/while/body/eval_jaxpr/ppermute | solution.py:16
  835.9 15.5 %collective-permute-start.3 = (bf16[1,16,16,512]{3,2,1,0:T(8,128)(2,1)S(1)}, bf16[1,16,16,512]{3,2,1,0:T(8,128)(2,1)S(1)}, u32[]{:S(2)}, u32[]{:S(2)}) collective-permute-start(bf16[1,16,16,512]{3,2,1,0:T(8,128)(2,1)S(1)} %collective-permute-done.2), channel_id=1, source_target_pairs={{0,128},{32,160},{64,192},{96,224},{128,0},{160,32},{192,64},{224,... | collective-permute-start | bytes 786440 | tf_op jit(solution)/shard_map/while/body/eval_jaxpr/ppermute | solution.py:16
  875.7 92.0 %all-reduce.4.cloned.1.call-done = bf16[4,1,16,16,512]{4,3,2,1,0:T(8,128)(2,1)} async-done(((bf16[4,1,16,16,512]{4,3,2,1,0:T(8,128)(2,1)}), bf16[4,1,16,16,512]{4,3,2,1,0:T(8,128)(2,1)}) %all-reduce.4.cloned.1.call-update) | async-done | bytes 1048592 | tf_op jit(solution)/shard_map/psum | solution.py:38
  (360 shorter events, 543.5 us)
Async XLA Ops:
  6.5 58.5 %all-gather.8.cloned.1.call-start = ((), (), s32[]{:S(2)}) async-start(), calls=%async_computation.2 | async-start | bytes 1622016 | tf_op jit(solution)/shard_map/all_gather | solution.py:75
  7.3 121.2 %all-gather.4.cloned.1.call-start = ((), (), s32[]{:S(2)}) async-start(), calls=%async_computation | async-start | bytes 4866048 | tf_op jit(solution)/shard_map/all_gather | solution.py:73
  8.0 183.6 %all-gather.6.cloned.1.call-start = ((), (), s32[]{:S(2)}) async-start(), calls=%async_computation.1 | async-start | bytes 4866048 | tf_op jit(solution)/shard_map/all_gather | solution.py:74
  8.7 959.0 %all-reduce.4.cloned.1.call-start = ((), (), s32[]{:S(2)}) async-start(), calls=%async_computation.3 | async-start | bytes 2097152 | tf_op jit(solution)/shard_map/psum | solution.py:38
  292.0 10.9 %collective-permute-start.4 = (bf16[1,16,16,512]{3,2,1,0:T(8,128)(2,1)S(1)}, bf16[1,16,16,512]{3,2,1,0:T(8,128)(2,1)S(1)}, u32[]{:S(2)}, u32[]{:S(2)}) collective-permute-start(bf16[1,16,16,512]{3,2,1,0:T(8,128)(2,1)S(1)} %get-tuple-element.378), channel_id=1, source_target_pairs={{0,1},{1,2},{2,3},{3,4},{4,5},{5,6},{6,7},{7,8},{8,9},{9,10},{10,1... | collective-permute-start | bytes 786440 | tf_op jit(solution)/shard_map/while/body/eval_jaxpr/ppermute | solution.py:27
  293.9 13.4 %collective-permute-start.5 = (bf16[1,16,16,512]{3,2,1,0:T(8,128)(2,1)S(1)}, bf16[1,16,16,512]{3,2,1,0:T(8,128)(2,1)S(1)}, u32[]{:S(2)}, u32[]{:S(2)}) collective-permute-start(bf16[1,16,16,512]{3,2,1,0:T(8,128)(2,1)S(1)} %get-tuple-element.378), channel_id=1, source_target_pairs={{1,0},{2,1},{3,2},{4,3},{5,4},{6,5},{7,6},{8,7},{9,8},{10,9},{11,1... | collective-permute-start | bytes 786440 | tf_op jit(solution)/shard_map/while/body/eval_jaxpr/ppermute | solution.py:29
  355.3 10.8 %collective-permute-start.4 = (bf16[1,16,16,512]{3,2,1,0:T(8,128)(2,1)S(1)}, bf16[1,16,16,512]{3,2,1,0:T(8,128)(2,1)S(1)}, u32[]{:S(2)}, u32[]{:S(2)}) collective-permute-start(bf16[1,16,16,512]{3,2,1,0:T(8,128)(2,1)S(1)} %get-tuple-element.378), channel_id=1, source_target_pairs={{0,1},{1,2},{2,3},{3,4},{4,5},{5,6},{6,7},{7,8},{8,9},{9,10},{10,1... | collective-permute-start | bytes 786440 | tf_op jit(solution)/shard_map/while/body/eval_jaxpr/ppermute | solution.py:27
  357.3 13.4 %collective-permute-start.5 = (bf16[1,16,16,512]{3,2,1,0:T(8,128)(2,1)S(1)}, bf16[1,16,16,512]{3,2,1,0:T(8,128)(2,1)S(1)}, u32[]{:S(2)}, u32[]{:S(2)}) collective-permute-start(bf16[1,16,16,512]{3,2,1,0:T(8,128)(2,1)S(1)} %get-tuple-element.378), channel_id=1, source_target_pairs={{1,0},{2,1},{3,2},{4,3},{5,4},{6,5},{7,6},{8,7},{9,8},{10,9},{11,1... | collective-permute-start | bytes 786440 | tf_op jit(solution)/shard_map/while/body/eval_jaxpr/ppermute | solution.py:29
  419.2 10.8 %collective-permute-start.4 = (bf16[1,16,16,512]{3,2,1,0:T(8,128)(2,1)S(1)}, bf16[1,16,16,512]{3,2,1,0:T(8,128)(2,1)S(1)}, u32[]{:S(2)}, u32[]{:S(2)}) collective-permute-start(bf16[1,16,16,512]{3,2,1,0:T(8,128)(2,1)S(1)} %get-tuple-element.378), channel_id=1, source_target_pairs={{0,1},{1,2},{2,3},{3,4},{4,5},{5,6},{6,7},{7,8},{8,9},{9,10},{10,1... | collective-permute-start | bytes 786440 | tf_op jit(solution)/shard_map/while/body/eval_jaxpr/ppermute | solution.py:27
  421.2 13.3 %collective-permute-start.5 = (bf16[1,16,16,512]{3,2,1,0:T(8,128)(2,1)S(1)}, bf16[1,16,16,512]{3,2,1,0:T(8,128)(2,1)S(1)}, u32[]{:S(2)}, u32[]{:S(2)}) collective-permute-start(bf16[1,16,16,512]{3,2,1,0:T(8,128)(2,1)S(1)} %get-tuple-element.378), channel_id=1, source_target_pairs={{1,0},{2,1},{3,2},{4,3},{5,4},{6,5},{7,6},{8,7},{9,8},{10,9},{11,1... | collective-permute-start | bytes 786440 | tf_op jit(solution)/shard_map/while/body/eval_jaxpr/ppermute | solution.py:29
  491.1 18.7 %collective-permute-start = (bf16[1,16,16,512]{3,2,1,0:T(8,128)(2,1)}, bf16[1,16,16,512]{3,2,1,0:T(8,128)(2,1)S(1)}, u32[]{:S(2)}, u32[]{:S(2)}) collective-permute-start(bf16[1,16,16,512]{3,2,1,0:T(8,128)(2,1)} %get-tuple-element.343), channel_id=1, source_target_pairs={{0,32},{32,64},{64,96},{96,128},{128,160},{160,192},{192,224},{1,3... | collective-permute-start | bytes 786440 | tf_op jit(solution)/shard_map/while/body/eval_jaxpr/ppermute | solution.py:12
  510.8 11.3 %collective-permute-start.1 = (bf16[1,16,16,512]{3,2,1,0:T(8,128)(2,1)S(1)}, bf16[1,16,16,512]{3,2,1,0:T(8,128)(2,1)S(1)}, u32[]{:S(2)}, u32[]{:S(2)}) collective-permute-start(bf16[1,16,16,512]{3,2,1,0:T(8,128)(2,1)S(1)} %bitcast_select_fusion.2), channel_id=1, source_target_pairs={{0,32},{32,0},{64,96},{96,64},{128,160},{160,128},{192,224},{224,1... | collective-permute-start | bytes 786440 | tf_op jit(solution)/shard_map/while/body/eval_jaxpr/ppermute | solution.py:16
  540.6 13.0 %collective-permute-start.5 = (bf16[1,16,16,512]{3,2,1,0:T(8,128)(2,1)S(1)}, bf16[1,16,16,512]{3,2,1,0:T(8,128)(2,1)S(1)}, u32[]{:S(2)}, u32[]{:S(2)}) collective-permute-start(bf16[1,16,16,512]{3,2,1,0:T(8,128)(2,1)S(1)} %get-tuple-element.378), channel_id=1, source_target_pairs={{1,0},{2,1},{3,2},{4,3},{5,4},{6,5},{7,6},{8,7},{9,8},{10,9},{11,1... | collective-permute-start | bytes 786440 | tf_op jit(solution)/shard_map/while/body/eval_jaxpr/ppermute | solution.py:29
  562.9 21.5 %collective-permute-start.1 = (bf16[1,16,16,512]{3,2,1,0:T(8,128)(2,1)S(1)}, bf16[1,16,16,512]{3,2,1,0:T(8,128)(2,1)S(1)}, u32[]{:S(2)}, u32[]{:S(2)}) collective-permute-start(bf16[1,16,16,512]{3,2,1,0:T(8,128)(2,1)S(1)} %bitcast_select_fusion.2), channel_id=1, source_target_pairs={{0,32},{32,0},{64,96},{96,64},{128,160},{160,128},{192,224},{224,1... | collective-permute-start | bytes 786440 | tf_op jit(solution)/shard_map/while/body/eval_jaxpr/ppermute | solution.py:16
  603.8 12.2 %collective-permute-start.5 = (bf16[1,16,16,512]{3,2,1,0:T(8,128)(2,1)S(1)}, bf16[1,16,16,512]{3,2,1,0:T(8,128)(2,1)S(1)}, u32[]{:S(2)}, u32[]{:S(2)}) collective-permute-start(bf16[1,16,16,512]{3,2,1,0:T(8,128)(2,1)S(1)} %get-tuple-element.378), channel_id=1, source_target_pairs={{1,0},{2,1},{3,2},{4,3},{5,4},{6,5},{7,6},{8,7},{9,8},{10,9},{11,1... | collective-permute-start | bytes 786440 | tf_op jit(solution)/shard_map/while/body/eval_jaxpr/ppermute | solution.py:29
  637.9 16.8 %collective-permute-start.2 = (bf16[1,16,16,512]{3,2,1,0:T(8,128)(2,1)S(1)}, bf16[1,16,16,512]{3,2,1,0:T(8,128)(2,1)S(1)}, u32[]{:S(2)}, u32[]{:S(2)}) collective-permute-start(bf16[1,16,16,512]{3,2,1,0:T(8,128)(2,1)S(1)} %collective-permute-done.1), channel_id=1, source_target_pairs={{0,64},{32,96},{64,0},{96,32},{128,192},{160,224},{192,128},{224,1... | collective-permute-start | bytes 786440 | tf_op jit(solution)/shard_map/while/body/eval_jaxpr/ppermute | solution.py:16
  664.9 10.8 %collective-permute-start.4 = (bf16[1,16,16,512]{3,2,1,0:T(8,128)(2,1)S(1)}, bf16[1,16,16,512]{3,2,1,0:T(8,128)(2,1)S(1)}, u32[]{:S(2)}, u32[]{:S(2)}) collective-permute-start(bf16[1,16,16,512]{3,2,1,0:T(8,128)(2,1)S(1)} %get-tuple-element.378), channel_id=1, source_target_pairs={{0,1},{1,2},{2,3},{3,4},{4,5},{5,6},{6,7},{7,8},{8,9},{9,10},{10,1... | collective-permute-start | bytes 786440 | tf_op jit(solution)/shard_map/while/body/eval_jaxpr/ppermute | solution.py:27
  699.2 17.3 %collective-permute-start.2 = (bf16[1,16,16,512]{3,2,1,0:T(8,128)(2,1)S(1)}, bf16[1,16,16,512]{3,2,1,0:T(8,128)(2,1)S(1)}, u32[]{:S(2)}, u32[]{:S(2)}) collective-permute-start(bf16[1,16,16,512]{3,2,1,0:T(8,128)(2,1)S(1)} %collective-permute-done.1), channel_id=1, source_target_pairs={{0,64},{32,96},{64,0},{96,32},{128,192},{160,224},{192,128},{224,1... | collective-permute-start | bytes 786440 | tf_op jit(solution)/shard_map/while/body/eval_jaxpr/ppermute | solution.py:16
  727.6 10.8 %collective-permute-start.4 = (bf16[1,16,16,512]{3,2,1,0:T(8,128)(2,1)S(1)}, bf16[1,16,16,512]{3,2,1,0:T(8,128)(2,1)S(1)}, u32[]{:S(2)}, u32[]{:S(2)}) collective-permute-start(bf16[1,16,16,512]{3,2,1,0:T(8,128)(2,1)S(1)} %get-tuple-element.378), channel_id=1, source_target_pairs={{0,1},{1,2},{2,3},{3,4},{4,5},{5,6},{6,7},{7,8},{8,9},{9,10},{10,1... | collective-permute-start | bytes 786440 | tf_op jit(solution)/shard_map/while/body/eval_jaxpr/ppermute | solution.py:27
  729.6 13.1 %collective-permute-start.5 = (bf16[1,16,16,512]{3,2,1,0:T(8,128)(2,1)S(1)}, bf16[1,16,16,512]{3,2,1,0:T(8,128)(2,1)S(1)}, u32[]{:S(2)}, u32[]{:S(2)}) collective-permute-start(bf16[1,16,16,512]{3,2,1,0:T(8,128)(2,1)S(1)} %get-tuple-element.378), channel_id=1, source_target_pairs={{1,0},{2,1},{3,2},{4,3},{5,4},{6,5},{7,6},{8,7},{9,8},{10,9},{11,1... | collective-permute-start | bytes 786440 | tf_op jit(solution)/shard_map/while/body/eval_jaxpr/ppermute | solution.py:29
  767.6 23.5 %collective-permute-start.3 = (bf16[1,16,16,512]{3,2,1,0:T(8,128)(2,1)S(1)}, bf16[1,16,16,512]{3,2,1,0:T(8,128)(2,1)S(1)}, u32[]{:S(2)}, u32[]{:S(2)}) collective-permute-start(bf16[1,16,16,512]{3,2,1,0:T(8,128)(2,1)S(1)} %collective-permute-done.2), channel_id=1, source_target_pairs={{0,128},{32,160},{64,192},{96,224},{128,0},{160,32},{192,64},{224,... | collective-permute-start | bytes 786440 | tf_op jit(solution)/shard_map/while/body/eval_jaxpr/ppermute | solution.py:16
  793.6 13.3 %collective-permute-start.5 = (bf16[1,16,16,512]{3,2,1,0:T(8,128)(2,1)S(1)}, bf16[1,16,16,512]{3,2,1,0:T(8,128)(2,1)S(1)}, u32[]{:S(2)}, u32[]{:S(2)}) collective-permute-start(bf16[1,16,16,512]{3,2,1,0:T(8,128)(2,1)S(1)} %get-tuple-element.378), channel_id=1, source_target_pairs={{1,0},{2,1},{3,2},{4,3},{5,4},{6,5},{7,6},{8,7},{9,8},{10,9},{11,1... | collective-permute-start | bytes 786440 | tf_op jit(solution)/shard_map/while/body/eval_jaxpr/ppermute | solution.py:29
  835.9 20.8 %collective-permute-start.3 = (bf16[1,16,16,512]{3,2,1,0:T(8,128)(2,1)S(1)}, bf16[1,16,16,512]{3,2,1,0:T(8,128)(2,1)S(1)}, u32[]{:S(2)}, u32[]{:S(2)}) collective-permute-start(bf16[1,16,16,512]{3,2,1,0:T(8,128)(2,1)S(1)} %collective-permute-done.2), channel_id=1, source_target_pairs={{0,128},{32,160},{64,192},{96,224},{128,0},{160,32},{192,64},{224,... | collective-permute-start | bytes 786440 | tf_op jit(solution)/shard_map/while/body/eval_jaxpr/ppermute | solution.py:16
  859.2 13.3 %collective-permute-start.5 = (bf16[1,16,16,512]{3,2,1,0:T(8,128)(2,1)S(1)}, bf16[1,16,16,512]{3,2,1,0:T(8,128)(2,1)S(1)}, u32[]{:S(2)}, u32[]{:S(2)}) collective-permute-start(bf16[1,16,16,512]{3,2,1,0:T(8,128)(2,1)S(1)} %get-tuple-element.378), channel_id=1, source_target_pairs={{1,0},{2,1},{3,2},{4,3},{5,4},{6,5},{7,6},{8,7},{9,8},{10,9},{11,1... | collective-permute-start | bytes 786440 | tf_op jit(solution)/shard_map/while/body/eval_jaxpr/ppermute | solution.py:29
  (58 other events, 435.5 us)
Sparse Core Ops, SparseCore 0:
  10.0 55.0 all-gather.7
  67.7 60.6 all-gather.3
  131.1 60.4 all-gather.5
  875.8 91.8 all-reduce.3
where the time goes:
time: 978 us; the launch traced here: 976 us
  waiting for transfers between devices  577 us (59%)
  starting transfers between devices  273 us (28%)
  matrix products  46.2 us (5%)
  other arithmetic  32.5 us (3%)
  loops' own time  17.3 us (2%)
  local copies, waits for them, and re-layouts  17 us (2%)
  between operations  13.2 us (1%)
    ppermute x33, waiting for transfers between devices, partner(): lax.ppermute(shard, axis, [(i, i ^ 1 << bit) for i in range(lax.axis_size...  190 us
    ppermute x33, starting transfers between devices, partner(): lax.ppermute(shard, axis, [(i, i ^ 1 << bit) for i in range(lax.axis_size...  141 us
    psum x1, waiting for transfers between devices, broadcast(): return lax.psum(jnp.where(mine, shard, jnp.zeros_like(shard)), axis)  92 us
    ppermute x11, starting transfers between devices, extended_2(): lax.ppermute(head, axis, [((i + 1) % count, i) for i in range(ends)])  73.2 us
    all_gather x1, waiting for transfers between devices, on_device(): lax.all_gather(conv_first, 'frame', axis=2, tiled=True)  63.4 us
    all_gather x1, waiting for transfers between devices, on_device(): lax.all_gather(conv_second, 'frame', axis=2, tiled=True)  63.1 us
    all_gather x1, waiting for transfers between devices, on_device(): lax.all_gather(temporal, 'frame', axis=2, tiled=True)  56.3 us
    ppermute x11, waiting for transfers between devices, passed_along(): return lax.ppermute(shard, axis, pairs)  47.2 us
  transfers between devices with their start and end apart: 70, of which 70 were waited for; matrix products, arithmetic and copies ran while one was open for 1% of the time, Pallas kernels for 0%

commit v1 on v0

--- a/solution.py
+++ b/solution.py
@@ -71,7 +71,9 @@
     segment_id = lax.axis_index("segment")
     first_full, second_full, time_full = (
         lax.all_gather(conv_first, "frame", axis=2, tiled=True),
-        lax.all_gather(conv_second, "frame", axis=2, tiled=True),
+        jnp.concatenate(
+            lax.all_to_all(jnp.stack([conv_second] * lax.axis_size("frame")), "frame", 0, 0), axis=2
+        ),
         lax.all_gather(temporal, "frame", axis=2, tiled=True),
     )
     first_kernel = first_full[0]

time: 978 us -> 955 us (0.976)
  waiting for transfers between devices: 577 us -> 539 us
    all_to_all x0 -> x1, waiting for transfers between devices: none -> 116 us  [on_device(): lax.all_to_all(jnp.stack([conv_second] * lax.axis_size('frame')), 'frame'...]
    all_gather x1 -> x0, waiting for transfers between devices: 63.1 us -> none  [on_device(): lax.all_gather(conv_second, 'frame', axis=2, tiled=True)]
    all_gather x1, waiting for transfers between devices: 56.3 us -> 0.01 us  [on_device(): lax.all_gather(temporal, 'frame', axis=2, tiled=True)]
    all_gather x1, waiting for transfers between devices: 63.4 us -> 30.2 us  [on_device(): lax.all_gather(conv_first, 'frame', axis=2, tiled=True)]
    all_to_all x0 -> x1, starting transfers between devices: none -> 11.7 us  [on_device(): lax.all_to_all(jnp.stack([conv_second] * lax.axis_size('frame')), 'frame'...]
  transfers between devices with their start and end apart: 70 -> 70, of which waited for: 70 -> 69; matrix products, arithmetic and copies ran while one was open for 1% -> 2% of each run, Pallas kernels for 0% -> 0%
where the time goes in v1:
time: 955 us; the launch traced here: 953 us
  waiting for transfers between devices  539 us (56%)
  starting transfers between devices  280 us (29%)
  matrix products  46.3 us (5%)
  other arithmetic  32.5 us (3%)
  local copies, waits for them, and re-layouts  25.3 us (3%)
  loops' own time  15.7 us (2%)
  between operations  13.2 us (1%)
    ppermute x33, waiting for transfers between devices, partner(): lax.ppermute(shard, axis, [(i, i ^ 1 << bit) for i in range(lax.axis_size...  182 us
    ppermute x33, starting transfers between devices, partner(): lax.ppermute(shard, axis, [(i, i ^ 1 << bit) for i in range(lax.axis_size...  146 us
    all_to_all x1, waiting for transfers between devices, on_device(): lax.all_to_all(jnp.stack([conv_second] * lax.axis_size('frame')), 'frame'...  116 us
    psum x1, waiting for transfers between devices, broadcast(): return lax.psum(jnp.where(mine, shard, jnp.zeros_like(shard)), axis)  95.3 us
    ppermute x11, starting transfers between devices, extended_2(): lax.ppermute(head, axis, [((i + 1) % count, i) for i in range(ends)])  73.2 us
    ppermute x11, waiting for transfers between devices, passed_along(): return lax.ppermute(shard, axis, pairs)  47.5 us
    ppermute x11, waiting for transfers between devices, extended_2(): lax.ppermute(head, axis, [((i + 1) % count, i) for i in range(ends)])  40.1 us
    dot_general x72, matrix products, spatial(): jnp.dot(window, kernel[3 * row_shift + col_shift], preferred_element_type...  39.3 us
  transfers between devices with their start and end apart: 70, of which 69 were waited for; matrix products, arithmetic and copies ran while one was open for 2% of the time, Pallas kernels for 0%

profile of v1, /device:TPU:2, one launch (start us, length us, event | category | flops | bytes accessed | tf_op | source)
XLA Modules:
  0.0 952.6 jit_solution(14303400762992597241)
XLA Ops:
  10.9 11.7 %all-to-all-start = ((bf16[32,1,9,16,512]{4,3,2,1,0:T(8,128)(2,1)}), bf16[32,1,9,16,512]{4,3,2,1,0:T(8,128)(2,1)}, u32[]{:S(2)}, u32[]{:S(2)}) async-start(bf16[32,1,9,16,512]{4,3,2,1,0:T(8,128)(2,1)} %stack.2), calls=%async_computation | async-start | bytes 9437184 | tf_op jit(solution)/shard_map/all_to_all | solution.py:75
  23.4 116.5 %all-to-all-done = bf16[32,1,9,16,512]{4,3,2,1,0:T(8,128)(2,1)} async-done(((bf16[32,1,9,16,512]{4,3,2,1,0:T(8,128)(2,1)}), bf16[32,1,9,16,512]{4,3,2,1,0:T(8,128)(2,1)}, u32[]{:S(2)}, u32[]{:S(2)}) %all-to-all-start) | async-done | bytes 4718624 | tf_op jit(solution)/shard_map/all_to_all | solution.py:75
  145.1 30.2 %all-gather.3.cloned.1.call-done = bf16[1,9,512,512]{3,2,1,0:T(8,128)(2,1)} async-done(((bf16[1,9,16,512]{3,2,1,0:T(8,128)(2,1)}), bf16[1,9,512,512]{3,2,1,0:T(8,128)(2,1)}) %all-gather.3.cloned.1.call-update) | async-done | bytes 4718608 | tf_op jit(solution)/shard_map/all_gather | solution.py:73
  176.1 672.0 %while.16 = (s32[]{:T(128)}, bf16[1,16,16,512]{3,2,1,0:T(8,128)(2,1)}, bf16[4,1,16,16,512]{4,3,2,1,0:T(8,128)(2,1)S(1)}, bf16[4,1,16,16,512]{4,3,2,1,0:T(8,128)(...) while((s32[]{:T(128)}, ...), condition=%wide.region_5.6_spmd.clone, body=%wide.region_0.5_spmd.clone.sunk | while | flops 2825650176 | bytes 99615424 | solution.py:130
  229.3 7.0 conditional.7
  254.3 7.6 collective-permute-done.2
  262.6 7.2 collective-permute-done.3
  291.1 7.0 conditional.7
  325.8 7.4 collective-permute-done.3
  354.5 7.0 conditional.7
  381.6 7.7 collective-permute-done.2
  389.9 7.2 collective-permute-done.3
  418.4 7.0 conditional.7
  451.6 7.4 collective-permute-done.3
  474.1 14.5 %collective-permute-start = (bf16[1,16,16,512]{3,2,1,0:T(8,128)(2,1)}, bf16[1,16,16,512]{3,2,1,0:T(8,128)(2,1)S(1)}, u32[]{:S(2)}, u32[]{:S(2)}) collective-permute-start(bf16[1,16,16,512]{3,2,1,0:T(8,128)(2,1)} %get-tuple-element.343), channel_id=1, source_target_pairs={{0,32},{32,64},{64,96},{96,128},{128,160},{160,192},{192,224},{1,3... | collective-permute-start | bytes 786440 | tf_op jit(solution)/shard_map/while/body/eval_jaxpr/ppermute | solution.py:12
  493.8 7.5 collective-permute-start.1
  514.4 7.2 collective-permute-done.3
  545.9 17.8 %collective-permute-start.1 = (bf16[1,16,16,512]{3,2,1,0:T(8,128)(2,1)S(1)}, bf16[1,16,16,512]{3,2,1,0:T(8,128)(2,1)S(1)}, u32[]{:S(2)}, u32[]{:S(2)}) collective-permute-start(bf16[1,16,16,512]{3,2,1,0:T(8,128)(2,1)S(1)} %bitcast_select_fusion.2), channel_id=1, source_target_pairs={{0,32},{32,0},{64,96},{96,64},{128,160},{160,128},{192,224},{224,1... | collective-permute-start | bytes 786440 | tf_op jit(solution)/shard_map/while/body/eval_jaxpr/ppermute | solution.py:16
  576.9 7.2 collective-permute-done.3
  617.7 11.0 %collective-permute-start.2 = (bf16[1,16,16,512]{3,2,1,0:T(8,128)(2,1)S(1)}, bf16[1,16,16,512]{3,2,1,0:T(8,128)(2,1)S(1)}, u32[]{:S(2)}, u32[]{:S(2)}) collective-permute-start(bf16[1,16,16,512]{3,2,1,0:T(8,128)(2,1)S(1)} %collective-permute-done.1), channel_id=1, source_target_pairs={{0,64},{32,96},{64,0},{96,32},{128,192},{160,224},{192,128},{224,1... | collective-permute-start | bytes 786440 | tf_op jit(solution)/shard_map/while/body/eval_jaxpr/ppermute | solution.py:16
  677.5 14.3 %collective-permute-start.2 = (bf16[1,16,16,512]{3,2,1,0:T(8,128)(2,1)S(1)}, bf16[1,16,16,512]{3,2,1,0:T(8,128)(2,1)S(1)}, u32[]{:S(2)}, u32[]{:S(2)}) collective-permute-start(bf16[1,16,16,512]{3,2,1,0:T(8,128)(2,1)S(1)} %collective-permute-done.1), channel_id=1, source_target_pairs={{0,64},{32,96},{64,0},{96,32},{128,192},{160,224},{192,128},{224,1... | collective-permute-start | bytes 786440 | tf_op jit(solution)/shard_map/while/body/eval_jaxpr/ppermute | solution.py:16
  748.4 15.0 %collective-permute-start.3 = (bf16[1,16,16,512]{3,2,1,0:T(8,128)(2,1)S(1)}, bf16[1,16,16,512]{3,2,1,0:T(8,128)(2,1)S(1)}, u32[]{:S(2)}, u32[]{:S(2)}) collective-permute-start(bf16[1,16,16,512]{3,2,1,0:T(8,128)(2,1)S(1)} %collective-permute-done.2), channel_id=1, source_target_pairs={{0,128},{32,160},{64,192},{96,224},{128,0},{160,32},{192,64},{224,... | collective-permute-start | bytes 786440 | tf_op jit(solution)/shard_map/while/body/eval_jaxpr/ppermute | solution.py:16
  807.4 18.8 %collective-permute-start.3 = (bf16[1,16,16,512]{3,2,1,0:T(8,128)(2,1)S(1)}, bf16[1,16,16,512]{3,2,1,0:T(8,128)(2,1)S(1)}, u32[]{:S(2)}, u32[]{:S(2)}) collective-permute-start(bf16[1,16,16,512]{3,2,1,0:T(8,128)(2,1)S(1)} %collective-permute-done.2), channel_id=1, source_target_pairs={{0,128},{32,160},{64,192},{96,224},{128,0},{160,32},{192,64},{224,... | collective-permute-start | bytes 786440 | tf_op jit(solution)/shard_map/while/body/eval_jaxpr/ppermute | solution.py:16
  849.2 95.3 %all-reduce.4.cloned.1.call-done = bf16[4,1,16,16,512]{4,3,2,1,0:T(8,128)(2,1)} async-done(((bf16[4,1,16,16,512]{4,3,2,1,0:T(8,128)(2,1)}), bf16[4,1,16,16,512]{4,3,2,1,0:T(8,128)(2,1)}) %all-reduce.4.cloned.1.call-update) | async-done | bytes 1048592 | tf_op jit(solution)/shard_map/psum | solution.py:38
  (361 shorter events, 539.5 us)
Async XLA Ops:
  6.5 138.6 %all-gather.5.cloned.1.call-start = ((), (), s32[]{:S(2)}) async-start(), calls=%async_computation.2 | async-start | bytes 1622016 | tf_op jit(solution)/shard_map/all_gather | solution.py:77
  10.9 129.0 %all-to-all-start = ((bf16[32,1,9,16,512]{4,3,2,1,0:T(8,128)(2,1)}), bf16[32,1,9,16,512]{4,3,2,1,0:T(8,128)(2,1)}, u32[]{:S(2)}, u32[]{:S(2)}) async-start(bf16[32,1,9,16,512]{4,3,2,1,0:T(8,128)(2,1)} %stack.2), calls=%async_computation | async-start | bytes 9437184 | tf_op jit(solution)/shard_map/all_to_all | solution.py:75
  22.6 152.8 %all-gather.3.cloned.1.call-start = ((), (), s32[]{:S(2)}) async-start(), calls=%async_computation.1 | async-start | bytes 4866048 | tf_op jit(solution)/shard_map/all_gather | solution.py:73
  23.4 921.2 %all-reduce.4.cloned.1.call-start = ((), (), s32[]{:S(2)}) async-start(), calls=%async_computation.3 | async-start | bytes 2097152 | tf_op jit(solution)/shard_map/psum | solution.py:38
  275.8 10.9 %collective-permute-start.4 = (bf16[1,16,16,512]{3,2,1,0:T(8,128)(2,1)S(1)}, bf16[1,16,16,512]{3,2,1,0:T(8,128)(2,1)S(1)}, u32[]{:S(2)}, u32[]{:S(2)}) collective-permute-start(bf16[1,16,16,512]{3,2,1,0:T(8,128)(2,1)S(1)} %get-tuple-element.378), channel_id=1, source_target_pairs={{0,1},{1,2},{2,3},{3,4},{4,5},{5,6},{6,7},{7,8},{8,9},{9,10},{10,1... | collective-permute-start | bytes 786440 | tf_op jit(solution)/shard_map/while/body/eval_jaxpr/ppermute | solution.py:27
  277.7 13.4 %collective-permute-start.5 = (bf16[1,16,16,512]{3,2,1,0:T(8,128)(2,1)S(1)}, bf16[1,16,16,512]{3,2,1,0:T(8,128)(2,1)S(1)}, u32[]{:S(2)}, u32[]{:S(2)}) collective-permute-start(bf16[1,16,16,512]{3,2,1,0:T(8,128)(2,1)S(1)} %get-tuple-element.378), channel_id=1, source_target_pairs={{1,0},{2,1},{3,2},{4,3},{5,4},{6,5},{7,6},{8,7},{9,8},{10,9},{11,1... | collective-permute-start | bytes 786440 | tf_op jit(solution)/shard_map/while/body/eval_jaxpr/ppermute | solution.py:29
  341.1 13.4 %collective-permute-start.5 = (bf16[1,16,16,512]{3,2,1,0:T(8,128)(2,1)S(1)}, bf16[1,16,16,512]{3,2,1,0:T(8,128)(2,1)S(1)}, u32[]{:S(2)}, u32[]{:S(2)}) collective-permute-start(bf16[1,16,16,512]{3,2,1,0:T(8,128)(2,1)S(1)} %get-tuple-element.378), channel_id=1, source_target_pairs={{1,0},{2,1},{3,2},{4,3},{5,4},{6,5},{7,6},{8,7},{9,8},{10,9},{11,1... | collective-permute-start | bytes 786440 | tf_op jit(solution)/shard_map/while/body/eval_jaxpr/ppermute | solution.py:29
  405.1 13.3 %collective-permute-start.5 = (bf16[1,16,16,512]{3,2,1,0:T(8,128)(2,1)S(1)}, bf16[1,16,16,512]{3,2,1,0:T(8,128)(2,1)S(1)}, u32[]{:S(2)}, u32[]{:S(2)}) collective-permute-start(bf16[1,16,16,512]{3,2,1,0:T(8,128)(2,1)S(1)} %get-tuple-element.378), channel_id=1, source_target_pairs={{1,0},{2,1},{3,2},{4,3},{5,4},{6,5},{7,6},{8,7},{9,8},{10,9},{11,1... | collective-permute-start | bytes 786440 | tf_op jit(solution)/shard_map/while/body/eval_jaxpr/ppermute | solution.py:29
  459.5 11.2 %collective-permute-start.4 = (bf16[1,16,16,512]{3,2,1,0:T(8,128)(2,1)S(1)}, bf16[1,16,16,512]{3,2,1,0:T(8,128)(2,1)S(1)}, u32[]{:S(2)}, u32[]{:S(2)}) collective-permute-start(bf16[1,16,16,512]{3,2,1,0:T(8,128)(2,1)S(1)} %get-tuple-element.378), channel_id=1, source_target_pairs={{0,1},{1,2},{2,3},{3,4},{4,5},{5,6},{6,7},{7,8},{8,9},{9,10},{10,1... | collective-permute-start | bytes 786440 | tf_op jit(solution)/shard_map/while/body/eval_jaxpr/ppermute | solution.py:27
  474.1 18.7 %collective-permute-start = (bf16[1,16,16,512]{3,2,1,0:T(8,128)(2,1)}, bf16[1,16,16,512]{3,2,1,0:T(8,128)(2,1)S(1)}, u32[]{:S(2)}, u32[]{:S(2)}) collective-permute-start(bf16[1,16,16,512]{3,2,1,0:T(8,128)(2,1)} %get-tuple-element.343), channel_id=1, source_target_pairs={{0,32},{32,64},{64,96},{96,128},{128,160},{160,192},{192,224},{1,3... | collective-permute-start | bytes 786440 | tf_op jit(solution)/shard_map/while/body/eval_jaxpr/ppermute | solution.py:12
  493.8 11.8 %collective-permute-start.1 = (bf16[1,16,16,512]{3,2,1,0:T(8,128)(2,1)S(1)}, bf16[1,16,16,512]{3,2,1,0:T(8,128)(2,1)S(1)}, u32[]{:S(2)}, u32[]{:S(2)}) collective-permute-start(bf16[1,16,16,512]{3,2,1,0:T(8,128)(2,1)S(1)} %bitcast_select_fusion.2), channel_id=1, source_target_pairs={{0,32},{32,0},{64,96},{96,64},{128,160},{160,128},{192,224},{224,1... | collective-permute-start | bytes 786440 | tf_op jit(solution)/shard_map/while/body/eval_jaxpr/ppermute | solution.py:16
  524.2 13.2 %collective-permute-start.5 = (bf16[1,16,16,512]{3,2,1,0:T(8,128)(2,1)S(1)}, bf16[1,16,16,512]{3,2,1,0:T(8,128)(2,1)S(1)}, u32[]{:S(2)}, u32[]{:S(2)}) collective-permute-start(bf16[1,16,16,512]{3,2,1,0:T(8,128)(2,1)S(1)} %get-tuple-element.378), channel_id=1, source_target_pairs={{1,0},{2,1},{3,2},{4,3},{5,4},{6,5},{7,6},{8,7},{9,8},{10,9},{11,1... | collective-permute-start | bytes 786440 | tf_op jit(solution)/shard_map/while/body/eval_jaxpr/ppermute | solution.py:29
  545.9 22.1 %collective-permute-start.1 = (bf16[1,16,16,512]{3,2,1,0:T(8,128)(2,1)S(1)}, bf16[1,16,16,512]{3,2,1,0:T(8,128)(2,1)S(1)}, u32[]{:S(2)}, u32[]{:S(2)}) collective-permute-start(bf16[1,16,16,512]{3,2,1,0:T(8,128)(2,1)S(1)} %bitcast_select_fusion.2), channel_id=1, source_target_pairs={{0,32},{32,0},{64,96},{96,64},{128,160},{160,128},{192,224},{224,1... | collective-permute-start | bytes 786440 | tf_op jit(solution)/shard_map/while/body/eval_jaxpr/ppermute | solution.py:16
  586.6 13.0 %collective-permute-start.5 = (bf16[1,16,16,512]{3,2,1,0:T(8,128)(2,1)S(1)}, bf16[1,16,16,512]{3,2,1,0:T(8,128)(2,1)S(1)}, u32[]{:S(2)}, u32[]{:S(2)}) collective-permute-start(bf16[1,16,16,512]{3,2,1,0:T(8,128)(2,1)S(1)} %get-tuple-element.378), channel_id=1, source_target_pairs={{1,0},{2,1},{3,2},{4,3},{5,4},{6,5},{7,6},{8,7},{9,8},{10,9},{11,1... | collective-permute-start | bytes 786440 | tf_op jit(solution)/shard_map/while/body/eval_jaxpr/ppermute | solution.py:29
  617.7 17.5 %collective-permute-start.2 = (bf16[1,16,16,512]{3,2,1,0:T(8,128)(2,1)S(1)}, bf16[1,16,16,512]{3,2,1,0:T(8,128)(2,1)S(1)}, u32[]{:S(2)}, u32[]{:S(2)}) collective-permute-start(bf16[1,16,16,512]{3,2,1,0:T(8,128)(2,1)S(1)} %collective-permute-done.1), channel_id=1, source_target_pairs={{0,64},{32,96},{64,0},{96,32},{128,192},{160,224},{192,128},{224,1... | collective-permute-start | bytes 786440 | tf_op jit(solution)/shard_map/while/body/eval_jaxpr/ppermute | solution.py:16
  646.6 13.3 %collective-permute-start.5 = (bf16[1,16,16,512]{3,2,1,0:T(8,128)(2,1)S(1)}, bf16[1,16,16,512]{3,2,1,0:T(8,128)(2,1)S(1)}, u32[]{:S(2)}, u32[]{:S(2)}) collective-permute-start(bf16[1,16,16,512]{3,2,1,0:T(8,128)(2,1)S(1)} %get-tuple-element.378), channel_id=1, source_target_pairs={{1,0},{2,1},{3,2},{4,3},{5,4},{6,5},{7,6},{8,7},{9,8},{10,9},{11,1... | collective-permute-start | bytes 786440 | tf_op jit(solution)/shard_map/while/body/eval_jaxpr/ppermute | solution.py:29
  677.5 21.2 %collective-permute-start.2 = (bf16[1,16,16,512]{3,2,1,0:T(8,128)(2,1)S(1)}, bf16[1,16,16,512]{3,2,1,0:T(8,128)(2,1)S(1)}, u32[]{:S(2)}, u32[]{:S(2)}) collective-permute-start(bf16[1,16,16,512]{3,2,1,0:T(8,128)(2,1)S(1)} %collective-permute-done.1), channel_id=1, source_target_pairs={{0,64},{32,96},{64,0},{96,32},{128,192},{160,224},{192,128},{224,1... | collective-permute-start | bytes 786440 | tf_op jit(solution)/shard_map/while/body/eval_jaxpr/ppermute | solution.py:16
  707.1 11.1 %collective-permute-start.4 = (bf16[1,16,16,512]{3,2,1,0:T(8,128)(2,1)S(1)}, bf16[1,16,16,512]{3,2,1,0:T(8,128)(2,1)S(1)}, u32[]{:S(2)}, u32[]{:S(2)}) collective-permute-start(bf16[1,16,16,512]{3,2,1,0:T(8,128)(2,1)S(1)} %get-tuple-element.378), channel_id=1, source_target_pairs={{0,1},{1,2},{2,3},{3,4},{4,5},{5,6},{6,7},{7,8},{8,9},{9,10},{10,1... | collective-permute-start | bytes 786440 | tf_op jit(solution)/shard_map/while/body/eval_jaxpr/ppermute | solution.py:27
  709.0 13.3 %collective-permute-start.5 = (bf16[1,16,16,512]{3,2,1,0:T(8,128)(2,1)S(1)}, bf16[1,16,16,512]{3,2,1,0:T(8,128)(2,1)S(1)}, u32[]{:S(2)}, u32[]{:S(2)}) collective-permute-start(bf16[1,16,16,512]{3,2,1,0:T(8,128)(2,1)S(1)} %get-tuple-element.378), channel_id=1, source_target_pairs={{1,0},{2,1},{3,2},{4,3},{5,4},{6,5},{7,6},{8,7},{9,8},{10,9},{11,1... | collective-permute-start | bytes 786440 | tf_op jit(solution)/shard_map/while/body/eval_jaxpr/ppermute | solution.py:29
  748.4 19.4 %collective-permute-start.3 = (bf16[1,16,16,512]{3,2,1,0:T(8,128)(2,1)S(1)}, bf16[1,16,16,512]{3,2,1,0:T(8,128)(2,1)S(1)}, u32[]{:S(2)}, u32[]{:S(2)}) collective-permute-start(bf16[1,16,16,512]{3,2,1,0:T(8,128)(2,1)S(1)} %collective-permute-done.2), channel_id=1, source_target_pairs={{0,128},{32,160},{64,192},{96,224},{128,0},{160,32},{192,64},{224,... | collective-permute-start | bytes 786440 | tf_op jit(solution)/shard_map/while/body/eval_jaxpr/ppermute | solution.py:16
  768.3 12.6 %collective-permute-start.4 = (bf16[1,16,16,512]{3,2,1,0:T(8,128)(2,1)S(1)}, bf16[1,16,16,512]{3,2,1,0:T(8,128)(2,1)S(1)}, u32[]{:S(2)}, u32[]{:S(2)}) collective-permute-start(bf16[1,16,16,512]{3,2,1,0:T(8,128)(2,1)S(1)} %get-tuple-element.378), channel_id=1, source_target_pairs={{0,1},{1,2},{2,3},{3,4},{4,5},{5,6},{6,7},{7,8},{8,9},{9,10},{10,1... | collective-permute-start | bytes 786440 | tf_op jit(solution)/shard_map/while/body/eval_jaxpr/ppermute | solution.py:27
  770.3 13.1 %collective-permute-start.5 = (bf16[1,16,16,512]{3,2,1,0:T(8,128)(2,1)S(1)}, bf16[1,16,16,512]{3,2,1,0:T(8,128)(2,1)S(1)}, u32[]{:S(2)}, u32[]{:S(2)}) collective-permute-start(bf16[1,16,16,512]{3,2,1,0:T(8,128)(2,1)S(1)} %get-tuple-element.378), channel_id=1, source_target_pairs={{1,0},{2,1},{3,2},{4,3},{5,4},{6,5},{7,6},{8,7},{9,8},{10,9},{11,1... | collective-permute-start | bytes 786440 | tf_op jit(solution)/shard_map/while/body/eval_jaxpr/ppermute | solution.py:29
  807.4 23.1 %collective-permute-start.3 = (bf16[1,16,16,512]{3,2,1,0:T(8,128)(2,1)S(1)}, bf16[1,16,16,512]{3,2,1,0:T(8,128)(2,1)S(1)}, u32[]{:S(2)}, u32[]{:S(2)}) collective-permute-start(bf16[1,16,16,512]{3,2,1,0:T(8,128)(2,1)S(1)} %collective-permute-done.2), channel_id=1, source_target_pairs={{0,128},{32,160},{64,192},{96,224},{128,0},{160,32},{192,64},{224,... | collective-permute-start | bytes 786440 | tf_op jit(solution)/shard_map/while/body/eval_jaxpr/ppermute | solution.py:16
  833.0 13.1 %collective-permute-start.5 = (bf16[1,16,16,512]{3,2,1,0:T(8,128)(2,1)S(1)}, bf16[1,16,16,512]{3,2,1,0:T(8,128)(2,1)S(1)}, u32[]{:S(2)}, u32[]{:S(2)}) collective-permute-start(bf16[1,16,16,512]{3,2,1,0:T(8,128)(2,1)S(1)} %get-tuple-element.378), channel_id=1, source_target_pairs={{1,0},{2,1},{3,2},{4,3},{5,4},{6,5},{7,6},{8,7},{9,8},{10,9},{11,1... | collective-permute-start | bytes 786440 | tf_op jit(solution)/shard_map/while/body/eval_jaxpr/ppermute | solution.py:29
  (58 other events, 418.0 us)
Sparse Core Ops, SparseCore 0:
  10.0 79.8 all-gather.4
  92.6 82.7 all-gather.2
  849.3 95.1 all-reduce.3
